TPU v7x, 32 devices: a whole 2x2x4 slice. The times are simulated.
32 devices in a mesh: lat: 8 (over z, x), fld: 4 (over y, core).
Axes of the slice: x: 2, y: 2, z: 4, core: 2. Of those that a mesh axis runs over, the one named last changes fastest.
Arguments:
- field_grid: bfloat16 [8, 2560, 5120], P('fld', 'lat'), may hold values from -300 to 300
- wave_table: int32 [64], replicated, may hold values from 0 to 1279, as said below
- legendre: bfloat16 [64, 2, 640, 1280], P('lat', None, 'fld'), may hold values from -0.15625 to 0.15625
Outputs:
- spectral: float32 [64, 640, 32], P('lat', 'fld')
Inputs may be any that keep to these rules, and one draw needn't show every extreme that they name: `wave_table`: the entries differ from one another; each aligned block of 8 entries owned by one index of lat is made of pairs m and 1279 - m, next to each other.
All inputs are finite; a program needn't handle non-finite values.
Results may differ from a plain program's by a relative error of at most 0.0048.
Values may be sent and summed in bfloat16 or wider, within the bound.
A program may use at most 64 MiB of HBM per device.

v0:
```python
import math

import jax
import jax.numpy as jnp
from jax import lax
from jax.sharding import PartitionSpec as P

TWO_PI = 2.0 * math.pi


def twiddle_block(wave_block, lon_total):
    fine_count = math.gcd(lon_total, 128)
    coarse_count = lon_total // fine_count
    waves = wave_block[:, None]
    coarse_index = (
        waves * (jnp.arange(coarse_count, dtype=jnp.int32) * fine_count)[None, :] % lon_total
    )
    fine_index = waves * jnp.arange(fine_count, dtype=jnp.int32)[None, :] % lon_total
    coarse_angle = coarse_index.astype(jnp.float32) * (TWO_PI / lon_total)
    fine_angle = fine_index.astype(jnp.float32) * (TWO_PI / lon_total)
    coarse_cos = jnp.cos(coarse_angle)[:, :, None]
    coarse_sin = jnp.sin(coarse_angle)[:, :, None]
    fine_cos = jnp.cos(fine_angle)[:, None, :]
    fine_sin = jnp.sin(fine_angle)[:, None, :]
    cosine = (coarse_cos * fine_cos - coarse_sin * fine_sin).reshape(wave_block.shape[0], lon_total)
    minus_sine = (-(coarse_sin * fine_cos + coarse_cos * fine_sin)).reshape(
        wave_block.shape[0], lon_total
    )
    return jnp.concatenate([cosine, minus_sine], axis=0).astype(jnp.bfloat16)


def fold_halves(fourier):
    half_lat = fourier.shape[-1] // 2
    north_rows = fourier[..., :half_lat].astype(jnp.float32)
    south_rows = jnp.flip(fourier[..., half_lat:], axis=-1).astype(jnp.float32)
    return jnp.stack([north_rows + south_rows, north_rows - south_rows], axis=1).astype(
        jnp.bfloat16
    )


def shards(field_grid, wave_table, legendre):
    f_dev, lat_dev, lon_total = field_grid.shape
    slot_total = wave_table.shape[0]
    slot_dev = legendre.shape[0]
    row_dev = legendre.shape[2]
    grid_rows = field_grid.reshape(f_dev * lat_dev, lon_total)
    block_size = math.gcd(slot_total, 256)
    wave_blocks = wave_table.reshape(slot_total // block_size, block_size)

    def transform(wave_block):
        twiddle = twiddle_block(wave_block, lon_total)
        spectra = lax.dot_general(
            twiddle, grid_rows, (((1,), (1,)), ((), ())), preferred_element_type=jnp.float32
        )
        spectra = (spectra * (1.0 / lon_total)).astype(jnp.bfloat16)
        return jnp.transpose(spectra.reshape(2, block_size, f_dev, lat_dev), (1, 0, 2, 3))

    fourier = lax.map(transform, wave_blocks).reshape(slot_total, 2, f_dev, lat_dev)
    first_slot = lax.axis_index("lat") * slot_dev
    own_waves = lax.dynamic_slice_in_dim(wave_table, first_slot, slot_dev)
    trunc_total = 2 * row_dev * lax.axis_size("fld")
    row_index = lax.axis_index("fld") * row_dev + jnp.arange(row_dev, dtype=jnp.int32)
    parity = jnp.arange(2, dtype=jnp.int32)
    degree = own_waves[:, None, None] + 2 * row_index[None, :, None] + parity[None, None, :]
    valid_mask = (degree <= trunc_total - 1).astype(jnp.float32)
    regrouped = lax.all_to_all(fourier, "lat", split_axis=0, concat_axis=3, tiled=True)
    folded = fold_halves(regrouped)
    folded_piece = lax.all_gather(folded, "fld", axis=3, tiled=True)
    parts_count = folded_piece.shape[2]
    width = folded_piece.shape[3]
    merged = folded_piece.reshape(slot_dev, 2, parts_count * width, folded_piece.shape[4])
    coeffs = jnp.einsum("sprj,spcj->srpc", legendre, merged, preferred_element_type=jnp.float32)
    coeffs = coeffs.reshape(slot_dev, row_dev, 2, parts_count, width)
    coeffs = coeffs * valid_mask[:, :, :, None, None]
    return coeffs.reshape(slot_dev, row_dev, -1)


def solution(mesh):
    placed = (P("fld", "lat", None), P(), P("lat", None, "fld", None))
    return jax.shard_map(
        shards, mesh=mesh, in_specs=placed, out_specs=P("lat", "fld", None), check_vma=False
    )
```

profile of v0, /device:TPU:1, one launch (start us, length us, event | category | flops | bytes accessed | tf_op | source)
XLA Modules:
  0.0 38.4 jit_solution(13432948485033546374)
XLA Ops:
  0.0 0.9 %fusion.24 = (f32[64,128]{1,0:T(8,128)S(1)}, f32[64,128]{1,0:T(8,128)S(1)}) fusion(s32[64]{0:T(128)} %param.4), kind=kLoop, calls=%fused_computation.32 | loop fusion | flops 73728 | bytes 65792 | tf_op jit(solution)/shard_map/while/body/eval_jaxpr/cos | solution.py:23
  0.9 0.9 %fusion.28 = (f32[64,40]{1,0:T(8,128)S(1)}, f32[64,40]{1,0:T(8,128)S(1)}) fusion(s32[40]{0:T(128)S(1)} %iota_multiply_fusion, s32[64]{0:T(128)} %param.4), kind=kLoop, calls=%fused_computation.37 | loop fusion | flops 23040 | bytes 20896 | tf_op jit(solution)/shard_map/while/body/eval_jaxpr/cos | solution.py:21
  1.8 0.8 %subtract_convert_fusion = (bf16[64,40,128]{2,1,0:T(8,128)(2,1)S(1)}, bf16[64,40,128]{2,1,0:T(8,128)(2,1)S(1)}) fusion(f32[64,128]{1,0:T(8,128)S(1)} %get-tuple-element.24, f32[64,40]{1,0:T(8,128)S(1)} %get-tuple-element.22, f32[64,128]{1,0:T(8,128)S(1)} %get-tuple-element.23, f32[64,40]{1,0:T(8,128)S(1)} %get-tuple-element.21), kind=kLoop, calls=%fused_computation.5 | loop fusion | flops 2949120 | bytes 1396736 | tf_op jit(solution)/shard_map/convert.7
  2.6 0.2 copy_bitcast_fusion
  2.8 0.0 copy-start
  2.8 5.0 %fusion.7 = bf16[128,640]{1,0:T(8,128)(2,1)S(1)} fusion(bf16[640,5120]{1,0:T(8,128)(2,1)} %bitcast.37, bf16[64,5120]{1,0:T(8,128)(2,1)S(1)} %get-tuple-element.25, bf16[64,5120]{1,0:T(8,128)(2,1)S(1)} %get-tuple-element.26), kind=kOutput, calls=%fused_computation.7 | convolution fusion | flops 841646080 | bytes 8028160 | tf_op jit(solution)/shard_map/while/body/eval_jaxpr/dot_general | solution.py:52
  7.8 0.2 reshape.193
  8.0 0.8 %copy.19 = bf16[2,64,2,320]{3,2,0,1:T(2,128)(2,1)} copy(bf16[2,64,2,320]{3,2,1,0:T(2,128)(2,1)S(1)} %reshape.193) | data formatting | bytes 327680 | tf_op jit(solution)/shard_map/while/body/eval_jaxpr/reshape | solution.py:56
  8.8 6.3 %all-to-all-start = ((bf16[64,2,2,320]{3,2,1,0:T(2,128)(2,1)}), bf16[64,2,2,320]{3,2,1,0:T(2,128)(2,1)S(1)}, u32[]{:S(2)}, u32[]{:S(2)}) async-start(bf16[64,2,2,320]{3,2,1,0:T(2,128)(2,1)} %bitcast.33), calls=%async_computation | async-start | bytes 393216 | tf_op jit(solution)/shard_map/all_to_all | solution.py:66
  15.2 0.0 copy-done
  15.2 0.1 dynamic_slice.6
  15.2 0.1 broadcast_add_fusion
  15.3 6.5 %all-to-all-done = bf16[64,2,2,320]{3,2,1,0:T(2,128)(2,1)S(1)} async-done(((bf16[64,2,2,320]{3,2,1,0:T(2,128)(2,1)}), bf16[64,2,2,320]{3,2,1,0:T(2,128)(2,1)S(1)}, u32[]{:S(2)}, u32[]{:S(2)}) %all-to-all-start) | async-done | bytes 163872 | tf_op jit(solution)/shard_map/all_to_all | solution.py:66
  21.8 0.1 copy.7
  21.9 0.2 all_to_all.16
  22.0 0.8 %rev.4 = bf16[8,2,2,1280]{3,0,1,2:T(8,128)(2,1)S(1)} reverse(bf16[8,2,2,1280]{3,0,1,2:T(8,128)(2,1)S(1)} %slice.9), dimensions={3} | reverse | bytes 163840 | tf_op jit(solution)/shard_map/jit(_flip)/rev | solution.py:35
  22.9 10.0 %all_gather.3 = bf16[8,2,2,8,1280]{4,0,2,1,3:T(8,128)(2,1)S(1)} all-gather(bf16[8,2,2,2,1280]{4,0,2,1,3:T(8,128)(2,1)S(1)} %pad_maximum_fusion), channel_id=1, replica_groups=mesh['lat'=8,'fld'=4] {'fld'}, dimensions={3}, use_global_device_ids=true | all-gather | bytes 819200 | tf_op jit(solution)/shard_map/all_gather | solution.py:68
  33.0 4.7 %fusion.10 = f32[8,2,16,160]{3,2,1,0:T(8,128)S(1)} fusion(bf16[8,2,160,1280]{3,2,1,0:T(8,128)(2,1)} %param.5, bf16[8,2,2,8,1280]{4,0,2,1,3:T(8,128)(2,1)S(1)} %all_gather.3), kind=kOutput, calls=%fused_computation.10 | convolution fusion | flops 104857600 | bytes 7372800 | tf_op jit(solution)/shard_map/sprj,spcj->srpc/dot_general | solution.py:72
  37.6 0.8 %bitcast_multiply_fusion = f32[8,160,32]{1,2,0:T(8,128)} fusion(f32[8,2,16,160]{3,2,1,0:T(8,128)S(1)} %fusion.10, f32[8,160,2]{1,2,0:T(2,128)S(1)} %compare_convert_fusion), kind=kLoop, calls=%fused_computation.13 | loop fusion | flops 40960 | bytes 337920 | tf_op jit(solution)/shard_map/mul | solution.py:74
  (6 shorter events, 0.1 us)
Async XLA Ops:
  2.8 12.4 %copy-start = (s32[64]{0:T(128)S(1)}, s32[64]{0:T(128)}, u32[]{:S(2)}) copy-start(s32[64]{0:T(128)} %param.4) | copy-start | bytes 772
  8.8 13.0 %all-to-all-start = ((bf16[64,2,2,320]{3,2,1,0:T(2,128)(2,1)}), bf16[64,2,2,320]{3,2,1,0:T(2,128)(2,1)S(1)}, u32[]{:S(2)}, u32[]{:S(2)}) async-start(bf16[64,2,2,320]{3,2,1,0:T(2,128)(2,1)} %bitcast.33), calls=%async_computation | async-start | bytes 393216 | tf_op jit(solution)/shard_map/all_to_all | solution.py:66
where the time goes:
time: 38.8 us; the launch traced here: 38.4 us
  blocking collectives  10 us (26%)
  matrix products  9.67 us (25%)
  waiting for transfers between devices  6.46 us (17%)
  starting transfers between devices  6.34 us (16%)
  other arithmetic  3.49 us (9%)
  local copies, waits for them, and re-layouts  2.32 us (6%)
    all_gather x1, blocking collectives, shards(): folded_piece = lax.all_gather(folded, 'fld', axis=3, tiled=True)  10 us
    all_to_all x1, waiting for transfers between devices, shards(): lax.all_to_all(fourier, 'lat', split_axis=0, concat_axis=3, tiled=True)  6.46 us
    all_to_all x1, starting transfers between devices, shards(): lax.all_to_all(fourier, 'lat', split_axis=0, concat_axis=3, tiled=True)  6.34 us
    dot_general x1, matrix products, transform(): lax.dot_general(twiddle, grid_rows, (((1,), (1,)), ((), ())), preferred_e...  4.99 us
    dot_general x1, matrix products, shards(): jnp.einsum('sprj,spcj->srpc', legendre, merged, preferred_element_type=jn...  4.68 us
    reshape x2, local copies, waits for them, and re-layouts, transform(): spectra.reshape(2, block_size, f_dev, lat_dev)  1 us
    cos x1, other arithmetic, twiddle_block(): coarse_cos = jnp.cos(coarse_angle)[:, :, None]  0.87 us
    cos x1, other arithmetic, twiddle_block(): fine_cos = jnp.cos(fine_angle)[:, None, :]  0.87 us
  transfers between devices with their start and end apart: 1, of which 1 were waited for; matrix products, arithmetic and copies ran while one was open for 0% of the time, Pallas kernels for 0%

commit v1 on v0

--- a/solution.py
+++ b/solution.py
@@ -1,8 +1,11 @@
+import functools
 import math
 
 import jax
 import jax.numpy as jnp
 from jax import lax
+from jax.experimental import pallas as pl
+from jax.experimental.pallas import tpu as pltpu
 from jax.sharding import PartitionSpec as P
 
 TWO_PI = 2.0 * math.pi
@@ -38,7 +41,7 @@
     )
 
 
-def shards(field_grid, wave_table, legendre):
+def shards_by_collectives(field_grid, wave_table, legendre):
     f_dev, lat_dev, lon_total = field_grid.shape
     slot_total = wave_table.shape[0]
     slot_dev = legendre.shape[0]
@@ -75,6 +78,333 @@
     return coeffs.reshape(slot_dev, row_dev, -1)
 
 
+LANES = 128
+HALF = 64
+MESH = pl.DeviceIdType.MESH
+
+
+def sin_cos_of_phase(phase, period):
+    turns = jnp.floor(phase * (1.0 / period))
+    rest = phase - turns * period
+    rest = jnp.where(rest < 0, rest + period, rest)
+    rest = jnp.where(rest >= period, rest - period, rest)
+    eighth = period / 8
+    q0 = rest < eighth
+    q1 = rest < 3 * eighth
+    q2 = rest < 5 * eighth
+    q3 = rest < 7 * eighth
+    centre = jnp.where(
+        q0, 0.0, jnp.where(q1, 2 * eighth, jnp.where(q2, 4 * eighth, jnp.where(q3, 6 * eighth, period)))
+    )
+    x = (rest - centre) * (TWO_PI / period)
+    y = x * x
+    s = x * (1.0 + y * (-1 / 6 + y * (1 / 120 + y * (-1 / 5040 + y * (1 / 362880)))))
+    c = 1.0 + y * (-1 / 2 + y * (1 / 24 + y * (-1 / 720 + y * (1 / 40320 - y * (1 / 3628800)))))
+    even = q0 | (q2 & ~q1) | ~q3
+    minus_sin = (q3 & ~q1)
+    minus_cos = (q2 & ~q0)
+    sine = jnp.where(even, s, c)
+    sine = jnp.where(minus_sin, -sine, sine)
+    cosine = jnp.where(even, c, s)
+    cosine = jnp.where(minus_cos, -cosine, cosine)
+    return sine, cosine
+
+
+def transform_kernel(
+    lat_count, wave_scalar_ref, wave_row_ref, field_ref, legendre_ref, out_ref,
+    grid, twiddle, coarse, table, send, recv, folded, spun,
+    field_sem, table_sem, send_sem, recv_sem, y_send, y_recv, c_send, c_recv, d_send, d_recv,
+):
+    lat = lax.axis_index("lat")
+    fld = lax.axis_index("fld")
+    y_peer = (fld + 2) % 4
+    partner = fld + 1 - 2 * (fld % 2)
+    partner_y = (partner + 2) % 4
+
+    _, lat_dev, lon_total = field_ref.shape
+    main = lat_dev // LANES
+    tiles = 2 * main + 1
+    slot_dev, _, row_dev, _ = legendre_ref.shape
+    slot_total = wave_row_ref.shape[1]
+    half_lats = lat_count // 2
+
+    south = lat // half_lats
+    band = lat + south * (lat_count - 1 - 2 * lat)
+    odd = band % 2
+    mixed = (south + odd) % 2
+
+    barrier = pltpu.get_barrier_semaphore()
+    for d in range(1, lat_count):
+        pl.semaphore_signal(
+            barrier, inc=1, device_id=((lat + d) % lat_count, fld), device_id_type=MESH
+        )
+    for other in (y_peer, partner):
+        pl.semaphore_signal(barrier, inc=1, device_id=(lat, other), device_id_type=MESH)
+
+    loads = []
+
+    def load(f, row, count, dst):
+        k = len(loads)
+        copy = pltpu.make_async_copy(
+            field_ref.at[f, pl.ds(pl.multiple_of(row, HALF), count)],
+            grid.at[pl.ds(pl.multiple_of(dst, HALF), count)],
+            field_sem.at[k],
+        )
+        copy.start()
+        loads.append(copy)
+
+    def load_main(f, t, dst):
+        north_row = LANES * t + HALF * odd
+        south_row = lat_dev - LANES - LANES * t - HALF * odd
+        load(f, north_row + south * (south_row - north_row), LANES, dst)
+
+    for t in range(main):
+        load_main(0, t, LANES * t)
+    tail_row = (lat_dev - HALF) * (1 - mixed)
+    load(0, tail_row, HALF, LANES * main + HALF * mixed)
+    load(1, tail_row, HALF, LANES * main + HALF * (1 - mixed))
+    for t in range(main):
+        load_main(1, t, LANES * (main + 1 + t))
+
+    waves = wave_row_ref[...].astype(jnp.float32)
+    waves = jnp.concatenate([waves, waves], axis=1)
+    width = 2 * slot_total
+    coarse_count = lon_total // LANES
+    k_fine = lax.broadcasted_iota(jnp.int32, (LANES, width), 0).astype(jnp.float32)
+    is_sine = lax.broadcasted_iota(jnp.int32, (LANES, width), 1) >= slot_total
+    quarter = jnp.where(is_sine, lon_total / 4, 0.0)
+    fine_sin, fine_cos = sin_cos_of_phase(waves * k_fine + quarter, lon_total)
+    coarse_rows = coarse.shape[1]
+    k_coarse = lax.broadcasted_iota(jnp.int32, (coarse_rows, width), 0).astype(jnp.float32) * LANES
+    coarse_sin, coarse_cos = sin_cos_of_phase(waves * k_coarse, lon_total)
+    coarse[0] = coarse_sin
+    coarse[1] = coarse_cos
+    for a in range(coarse_count):
+        block = coarse[1, pl.ds(a, 1), :] * fine_cos - coarse[0, pl.ds(a, 1), :] * fine_sin
+        twiddle[pl.ds(a * LANES, LANES), :] = block.astype(jnp.bfloat16)
+
+    row = lax.broadcasted_iota(jnp.int32, (LANES, LANES), 0)
+    column = lax.broadcasted_iota(jnp.int32, (LANES, LANES), 1)
+    turned = row + south * (LANES - 1 - 2 * row)
+    order = (turned == column).astype(jnp.float32).astype(jnp.bfloat16)
+
+    chunk_tiles = ((0, main), (main, tiles))
+    chunk_loads = ((0, main), (main, len(loads)))
+    offsets = [d for pair in zip(range(lat_count // 2, 0, -1), range(lat_count // 2, lat_count)) for d in pair]
+    offsets = list(dict.fromkeys(offsets))
+
+    def columns(q):
+        low, high = chunk_tiles[q]
+        return pl.ds(low * LANES, (high - low) * LANES)
+
+    pending = []
+    for q in range(2):
+        for k in range(*chunk_loads[q]):
+            loads[k].wait()
+        low, high = chunk_tiles[q]
+        spectra = jnp.dot(
+            grid[pl.ds(low * LANES, (high - low) * LANES), :], twiddle[...],
+            preferred_element_type=jnp.float32,
+        )
+        spectra = (spectra * (1.0 / lon_total)).astype(jnp.bfloat16)
+        for t in range(low, high):
+            part = spectra[(t - low) * LANES:(t - low + 1) * LANES, :]
+            part = jnp.dot(order, part, preferred_element_type=jnp.float32)
+            part = part.T
+            for owner in range(lat_count):
+                s0 = owner * slot_dev
+                send[owner, :, pl.ds(t * LANES, LANES)] = jnp.concatenate(
+                    [part[s0:s0 + slot_dev], part[slot_total + s0:slot_total + s0 + slot_dev]], axis=0
+                ).astype(jnp.bfloat16)
+        if q == 0:
+            pl.semaphore_wait(barrier, lat_count + 1)
+        for d in offsets:
+            owner = (lat + d) % lat_count
+            copy = pltpu.make_async_remote_copy(
+                src_ref=send.at[owner, :, columns(q)],
+                dst_ref=recv.at[fld, lat, :, columns(q)],
+                send_sem=send_sem.at[d, q],
+                recv_sem=recv_sem.at[d, q],
+                device_id=(owner, fld),
+                device_id_type=MESH,
+            )
+            copy.start()
+            pending.append(copy)
+        for other, ss, rs in ((y_peer, y_send, y_recv), (partner, c_send, c_recv)):
+            copy = pltpu.make_async_remote_copy(
+                src_ref=send.at[lat, :, columns(q)],
+                dst_ref=recv.at[fld, lat, :, columns(q)],
+                send_sem=ss.at[0, q],
+                recv_sem=rs.at[0, q],
+                device_id=(lat, other),
+                device_id_type=MESH,
+            )
+            copy.start()
+            pending.append(copy)
+        recv[fld, lat, :, columns(q)] = send[lat, :, columns(q)]
+
+    table_copy = pltpu.make_async_copy(legendre_ref, table, table_sem)
+    table_copy.start()
+
+    near = list(reversed(offsets))
+    for q in range(2):
+        for d in near:
+            src = (lat + lat_count - d) % lat_count
+            here = recv.at[fld, src, :, columns(q)]
+            pltpu.make_async_remote_copy(
+                src_ref=here, dst_ref=here, send_sem=send_sem.at[d, q], recv_sem=recv_sem.at[d, q],
+                device_id=(lat, y_peer), device_id_type=MESH,
+            ).wait_recv()
+            for other, ss, rs in ((y_peer, y_send, y_recv), (partner, c_send, c_recv)):
+                copy = pltpu.make_async_remote_copy(
+                    src_ref=here, dst_ref=here, send_sem=ss.at[d, q], recv_sem=rs.at[d, q],
+                    device_id=(lat, other), device_id_type=MESH,
+                )
+                copy.start()
+                pending.append(copy)
+        for d in [0] + near:
+            src = (lat + lat_count - d) % lat_count
+            there = recv.at[y_peer, src, :, columns(q)]
+            pltpu.make_async_remote_copy(
+                src_ref=there, dst_ref=there, send_sem=y_send.at[d, q], recv_sem=y_recv.at[d, q],
+                device_id=(lat, y_peer), device_id_type=MESH,
+            ).wait_recv()
+            copy = pltpu.make_async_remote_copy(
+                src_ref=there, dst_ref=there, send_sem=d_send.at[d, q], recv_sem=d_recv.at[d, q],
+                device_id=(lat, partner), device_id_type=MESH,
+            )
+            copy.start()
+            pending.append(copy)
+    for q in range(2):
+        for d in [0] + near:
+            src = (lat + lat_count - d) % lat_count
+            for group, ss, rs in ((partner, c_send, c_recv), (partner_y, d_send, d_recv)):
+                place = recv.at[group, src, :, columns(q)]
+                pltpu.make_async_remote_copy(
+                    src_ref=place, dst_ref=place, send_sem=ss.at[d, q], recv_sem=rs.at[d, q],
+                    device_id=(lat, partner), device_id_type=MESH,
+                ).wait_recv()
+
+    depth = 2 * slot_dev
+    pair_lats = 2 * lat_dev
+    low_half = lax.broadcasted_iota(jnp.int32, (depth, LANES), 1) < HALF
+    for h in range(half_lats // 2):
+        for group in range(4):
+            north = [recv[group, 2 * h + o].astype(jnp.float32) for o in range(2)]
+            mirror = [recv[group, lat_count - 1 - 2 * h - o].astype(jnp.float32) for o in range(2)]
+            for p in range(2):
+                even_band, odd_band = [
+                    n + m if p == 0 else n - m for n, m in zip(north, mirror)
+                ]
+                cut = main * LANES
+                mid_even = even_band[:, cut:cut + LANES]
+                mid_odd = odd_band[:, cut:cut + LANES]
+                mid = (
+                    jnp.where(low_half, mid_even, mid_odd),
+                    pltpu.roll(jnp.where(low_half, mid_odd, mid_even), HALF, 1),
+                )
+                for f in range(2):
+                    start = f * (cut + LANES)
+                    rows = pl.ds((2 * group + f) * depth, depth)
+                    base = h * pair_lats
+                    folded[p, rows, pl.ds(base, cut)] = even_band[:, start:start + cut].astype(jnp.bfloat16)
+                    folded[p, rows, pl.ds(base + cut, LANES)] = mid[f].astype(jnp.bfloat16)
+                    folded[p, rows, pl.ds(base + cut + LANES, cut)] = odd_band[
+                        :, start:start + cut
+                    ].astype(jnp.bfloat16)
+
+    table_copy.wait()
+    total_rows = 8 * depth
+    trunc_total = 2 * row_dev * 4
+    slot_of = lax.broadcasted_iota(jnp.int32, (row_dev, total_rows), 1) % slot_dev
+    degree_row = 2 * (lax.broadcasted_iota(jnp.int32, (row_dev, total_rows), 0) + fld * row_dev)
+    for p in range(2):
+        kept = jnp.zeros((row_dev, total_rows), jnp.float32)
+        for s in range(slot_dev):
+            sums = lax.dot_general(
+                table[s, p], folded[p], (((1,), (1,)), ((), ())), preferred_element_type=jnp.float32
+            )
+            wave = wave_scalar_ref[lat * slot_dev + s]
+            valid = (slot_of == s) & (degree_row + (wave + p) <= trunc_total - 1)
+            kept = jnp.where(valid, sums, kept)
+        padded = jnp.concatenate(
+            [kept, jnp.zeros((spun.shape[1] * LANES - row_dev, total_rows), jnp.float32)], axis=0
+        )
+        for t in range(spun.shape[1]):
+            spun[p, t] = padded[t * LANES:(t + 1) * LANES].T
+    for s in range(slot_dev):
+        for p in range(2):
+            for c in range(2):
+                for t in range(spun.shape[1]):
+                    kept_rows = min(LANES, row_dev - t * LANES)
+                    out_ref[s, pl.ds(p * 16 + c * 8, 8), pl.ds(t * LANES, kept_rows)] = spun[
+                        p, t, pl.ds(c * slot_dev + s, 8, stride=depth), :
+                    ][:, :kept_rows]
+    for copy in pending:
+        copy.wait_send()
+
+
+def shards_by_kernel(field_grid, wave_table, legendre):
+    f_dev, lat_dev, lon_total = field_grid.shape
+    slot_dev, _, row_dev, north_total = legendre.shape
+    slot_total = wave_table.shape[0]
+    lat_count = lax.axis_size("lat")
+    rows = f_dev * lat_dev
+    bf16, f32 = jnp.bfloat16, jnp.float32
+    dma = pltpu.SemaphoreType.DMA
+    padded_rows = -(-row_dev // LANES) * LANES
+    coarse_rows = -(-(lon_total // LANES) // 8) * 8
+    vmem, smem = pltpu.VMEM, pltpu.SMEM
+    pairs = (lat_count, 2)
+    out = pl.pallas_call(
+        functools.partial(transform_kernel, lat_count),
+        out_shape=jax.ShapeDtypeStruct((slot_dev, 32, row_dev), f32),
+        in_specs=[
+            pl.BlockSpec(memory_space=smem),
+            pl.BlockSpec(memory_space=vmem),
+            pl.BlockSpec(memory_space=pl.ANY),
+            pl.BlockSpec(memory_space=pl.ANY),
+        ],
+        out_specs=pl.BlockSpec(memory_space=vmem),
+        scratch_shapes=[
+            vmem((rows, lon_total), bf16),
+            vmem((lon_total, 2 * slot_total), bf16),
+            vmem((2, coarse_rows, 2 * slot_total), f32),
+            vmem(legendre.shape, bf16),
+            vmem((lat_count, 2 * slot_dev, rows), bf16),
+            vmem((4, lat_count, 2 * slot_dev, rows), bf16),
+            vmem((2, 16 * slot_dev, north_total), bf16),
+            vmem((2, padded_rows // LANES, 16 * slot_dev, LANES), f32),
+            dma((2 * (lat_dev // LANES) + 2,)),
+            dma(()),
+        ] + [dma(pairs)] * 8,
+        compiler_params=pltpu.CompilerParams(
+            collective_id=0, has_side_effects=True
+        ),
+    )(wave_table, wave_table.reshape(1, slot_total), field_grid, legendre)
+    return jnp.transpose(out, (0, 2, 1))
+
+
+def shards(field_grid, wave_table, legendre):
+    f_dev, lat_dev, lon_total = field_grid.shape
+    slot_dev, _, row_dev, _ = legendre.shape
+    slot_total = wave_table.shape[0]
+    fits = (
+        f_dev == 2
+        and slot_dev == 8
+        and 2 * slot_total == LANES
+        and lat_dev % LANES == HALF
+        and lax.axis_size("fld") == 4
+        and lax.axis_size("lat") % 4 == 0
+        and lon_total % LANES == 0
+        and row_dev % 8 == 0
+        and 2 * row_dev * 4 * lon_total < 2**24
+    )
+    if fits:
+        return shards_by_kernel(field_grid, wave_table, legendre)
+    return shards_by_collectives(field_grid, wave_table, legendre)
+
+
 def solution(mesh):
     placed = (P("fld", "lat", None), P(), P("lat", None, "fld", None))
     return jax.shard_map(

time: 38.8 us -> 26 us (0.67)
  Pallas kernels: 0 us -> 24.2 us
  blocking collectives: 10 us -> 0 us
  matrix products: 9.67 us -> 0 us
  waiting for transfers between devices: 6.46 us -> 0 us
  starting transfers between devices: 6.34 us -> 0 us
  other arithmetic: 3.49 us -> 0 us
  local copies, waits for them, and re-layouts: 2.32 us -> 1.67 us
    pallas_call x0 -> x1, Pallas kernels: none -> 24.2 us  [shards_by_kernel(): pl.pallas_call(functools.partial(transform_kernel, lat_count), out_shape=...]
    all_gather x1 -> x0, blocking collectives: 10 us -> none  [shards(): folded_piece = lax.all_gather(folded, 'fld', axis=3, tiled=True)]
    dot_general x2 -> x0, matrix products: 9.67 us -> none  [the longest x1 4.99 us: transform(): lax.dot_general(twiddle, grid_rows, (((1,), (1,)), ((), ())), preferred_e...]
    all_to_all x1 -> x0, waiting for transfers between devices: 6.46 us -> none  [shards(): lax.all_to_all(fourier, 'lat', split_axis=0, concat_axis=3, tiled=True)]
    all_to_all x1 -> x0, starting transfers between devices: 6.34 us -> none  [shards(): lax.all_to_all(fourier, 'lat', split_axis=0, concat_axis=3, tiled=True)]
    cos x2 -> x0, other arithmetic: 1.74 us -> none  [the longest x1 0.87 us: twiddle_block(): coarse_cos = jnp.cos(coarse_angle)[:, :, None]]
    unnamed x2 -> x1, local copies, waits for them, and re-layouts: 0.01 us -> 1.67 us
    reshape x2 -> x0, local copies, waits for them, and re-layouts: 1 us -> none  [transform(): spectra.reshape(2, block_size, f_dev, lat_dev)]
  transfers between devices with their start and end apart: 1 -> 0, of which waited for: 1 -> 0; matrix products, arithmetic and copies ran while one was open for 0% -> 0% of each run, Pallas kernels for 0% -> 0%
where the time goes in v1:
time: 26 us; the launch traced here: 25.9 us
  Pallas kernels  24.2 us (93%)
  local copies, waits for them, and re-layouts  1.67 us (6%)
    pallas_call x1, Pallas kernels, shards_by_kernel(): pl.pallas_call(functools.partial(transform_kernel, lat_count), out_shape=...  24.2 us
    unnamed x1, local copies, waits for them, and re-layouts  1.67 us

profile of v1, /device:TPU:1, one launch (start us, length us, event | category | flops | bytes accessed | tf_op | source)
XLA Modules:
  0.0 25.9 jit_solution(5543051382862698892)
XLA Ops:
  0.0 24.2 %shard_map.37 = f32[8,32,160]{2,1,0:T(8,128)} custom-call(s32[64]{0:T(128)} %wave_scalar_ref.1, s32[1,64]{1,0:T(1,128)} %bitcast.3, bf16[2,320,5120]{2,1,0:T(8,128)(2,1)} %field_ref.1, bf16[8,2,160,1280]{3,2,1,0:T(8,128)(2,1)} %legendre_ref.1), custom_call_target="tpu_custom_call" | custom-call | tf_op jit(solution)/shard_map/pallas_call | solution.py:359
  24.2 1.7 %copy.5 = f32[8,160,32]{1,2,0:T(8,128)} copy(f32[8,160,32]{1,2,0:T(8,128)} %bitcast.2) | data formatting | bytes 327680

commit v2 on v1

--- a/solution.py
+++ b/solution.py
@@ -190,8 +190,16 @@
 
     chunk_tiles = ((0, main), (main, tiles))
     chunk_loads = ((0, main), (main, len(loads)))
-    offsets = [d for pair in zip(range(lat_count // 2, 0, -1), range(lat_count // 2, lat_count)) for d in pair]
-    offsets = list(dict.fromkeys(offsets))
+    near = sorted(range(1, lat_count))
+    offsets = near[::-1]
+
+    def flipped(d):
+        index, bit = lat, 1
+        while bit < lat_count:
+            if d & bit:
+                index = index + bit * (1 - 2 * ((lat // bit) % 2))
+            bit *= 2
+        return index
 
     def columns(q):
         low, high = chunk_tiles[q]
@@ -219,7 +227,7 @@
         if q == 0:
             pl.semaphore_wait(barrier, lat_count + 1)
         for d in offsets:
-            owner = (lat + d) % lat_count
+            owner = flipped(d)
             copy = pltpu.make_async_remote_copy(
                 src_ref=send.at[owner, :, columns(q)],
                 dst_ref=recv.at[fld, lat, :, columns(q)],
@@ -246,10 +254,9 @@
     table_copy = pltpu.make_async_copy(legendre_ref, table, table_sem)
     table_copy.start()
 
-    near = list(reversed(offsets))
     for q in range(2):
         for d in near:
-            src = (lat + lat_count - d) % lat_count
+            src = flipped(d)
             here = recv.at[fld, src, :, columns(q)]
             pltpu.make_async_remote_copy(
                 src_ref=here, dst_ref=here, send_sem=send_sem.at[d, q], recv_sem=recv_sem.at[d, q],
@@ -262,8 +269,9 @@
                 )
                 copy.start()
                 pending.append(copy)
+    for q in range(2):
         for d in [0] + near:
-            src = (lat + lat_count - d) % lat_count
+            src = flipped(d)
             there = recv.at[y_peer, src, :, columns(q)]
             pltpu.make_async_remote_copy(
                 src_ref=there, dst_ref=there, send_sem=y_send.at[d, q], recv_sem=y_recv.at[d, q],
@@ -277,7 +285,7 @@
             pending.append(copy)
     for q in range(2):
         for d in [0] + near:
-            src = (lat + lat_count - d) % lat_count
+            src = flipped(d)
             for group, ss, rs in ((partner, c_send, c_recv), (partner_y, d_send, d_recv)):
                 place = recv.at[group, src, :, columns(q)]
                 pltpu.make_async_remote_copy(
@@ -358,7 +366,7 @@
     pairs = (lat_count, 2)
     out = pl.pallas_call(
         functools.partial(transform_kernel, lat_count),
-        out_shape=jax.ShapeDtypeStruct((slot_dev, 32, row_dev), f32),
+        out_shape=pltpu.VMEM((slot_dev, 32, row_dev), f32),
         in_specs=[
             pl.BlockSpec(memory_space=smem),
             pl.BlockSpec(memory_space=vmem),
@@ -395,7 +403,7 @@
         and 2 * slot_total == LANES
         and lat_dev % LANES == HALF
         and lax.axis_size("fld") == 4
-        and lax.axis_size("lat") % 4 == 0
+        and lax.axis_size("lat") in (4, 8, 16)
         and lon_total % LANES == 0
         and row_dev % 8 == 0
         and 2 * row_dev * 4 * lon_total < 2**24

time: 26 us -> 23.1 us (0.89)
  Pallas kernels: 24.2 us -> 22.2 us
  local copies, waits for them, and re-layouts: 1.67 us -> 0.71 us
    pallas_call x1, Pallas kernels: 24.2 us -> 22.2 us  [shards_by_kernel(): pl.pallas_call(functools.partial(transform_kernel, lat_count), out_shape=...]
    unnamed x1, local copies, waits for them, and re-layouts: 1.67 us -> 0.71 us
where the time goes in v2:
time: 23.1 us; the launch traced here: 22.9 us
  Pallas kernels  22.2 us (96%)
  local copies, waits for them, and re-layouts  0.71 us (3%)
    pallas_call x1, Pallas kernels, shards_by_kernel(): pl.pallas_call(functools.partial(transform_kernel, lat_count), out_shape=...  22.2 us
    unnamed x1, local copies, waits for them, and re-layouts  0.71 us

profile of v2, /device:TPU:1, one launch (start us, length us, event | category | flops | bytes accessed | tf_op | source)
XLA Modules:
  0.0 22.9 jit_solution(9387443538659971464)
XLA Ops:
  0.0 22.2 %shard_map.37 = f32[8,32,160]{2,1,0:T(8,128)S(1)} custom-call(s32[64]{0:T(128)} %wave_scalar_ref.1, s32[1,64]{1,0:T(1,128)} %bitcast.3, bf16[2,320,5120]{2,1,0:T(8,128)(2,1)} %field_ref.1, bf16[8,2,160,1280]{3,2,1,0:T(8,128)(2,1)} %legendre_ref.1), custom_call_target="tpu_custom_call" | custom-call | tf_op jit(solution)/shard_map/pallas_call | solution.py:367
  22.2 0.7 %copy.5 = f32[8,160,32]{1,2,0:T(8,128)} copy(f32[8,160,32]{1,2,0:T(8,128)S(1)} %bitcast.2) | data formatting | bytes 327680

commit v3 on v2

--- a/solution.py
+++ b/solution.py
@@ -188,8 +188,8 @@
     turned = row + south * (LANES - 1 - 2 * row)
     order = (turned == column).astype(jnp.float32).astype(jnp.bfloat16)
 
-    chunk_tiles = ((0, main), (main, tiles))
-    chunk_loads = ((0, main), (main, len(loads)))
+    chunk_tiles = ((0, main), (main, main + 1), (main + 1, tiles))
+    chunk_loads = ((0, main), (main, main + 2), (main + 2, len(loads)))
     near = sorted(range(1, lat_count))
     offsets = near[::-1]
 
@@ -206,7 +206,7 @@
         return pl.ds(low * LANES, (high - low) * LANES)
 
     pending = []
-    for q in range(2):
+    for q in range(3):
         for k in range(*chunk_loads[q]):
             loads[k].wait()
         low, high = chunk_tiles[q]
@@ -254,7 +254,7 @@
     table_copy = pltpu.make_async_copy(legendre_ref, table, table_sem)
     table_copy.start()
 
-    for q in range(2):
+    for q in range(3):
         for d in near:
             src = flipped(d)
             here = recv.at[fld, src, :, columns(q)]
@@ -269,7 +269,7 @@
                 )
                 copy.start()
                 pending.append(copy)
-    for q in range(2):
+    for q in range(3):
         for d in [0] + near:
             src = flipped(d)
             there = recv.at[y_peer, src, :, columns(q)]
@@ -283,7 +283,7 @@
             )
             copy.start()
             pending.append(copy)
-    for q in range(2):
+    for q in range(3):
         for d in [0] + near:
             src = flipped(d)
             for group, ss, rs in ((partner, c_send, c_recv), (partner_y, d_send, d_recv)):
@@ -363,7 +363,7 @@
     padded_rows = -(-row_dev // LANES) * LANES
     coarse_rows = -(-(lon_total // LANES) // 8) * 8
     vmem, smem = pltpu.VMEM, pltpu.SMEM
-    pairs = (lat_count, 2)
+    pairs = (lat_count, 3)
     out = pl.pallas_call(
         functools.partial(transform_kernel, lat_count),
         out_shape=pltpu.VMEM((slot_dev, 32, row_dev), f32),

time: 23.1 us -> 21.9 us (0.948)
  Pallas kernels: 22.2 us -> 21.1 us
    pallas_call x1, Pallas kernels: 22.2 us -> 21.1 us  [shards_by_kernel(): pl.pallas_call(functools.partial(transform_kernel, lat_count), out_shape=...]
where the time goes in v3:
time: 21.9 us; the launch traced here: 21.8 us
  Pallas kernels  21.1 us (96%)
  local copies, waits for them, and re-layouts  0.71 us (3%)
    pallas_call x1, Pallas kernels, shards_by_kernel(): pl.pallas_call(functools.partial(transform_kernel, lat_count), out_shape=...  21.1 us
    unnamed x1, local copies, waits for them, and re-layouts  0.71 us

profile of v3, /device:TPU:1, one launch (start us, length us, event | category | flops | bytes accessed | tf_op | source)
XLA Modules:
  0.0 21.8 jit_solution(13541048714291138058)
XLA Ops:
  0.0 21.1 %shard_map.37 = f32[8,32,160]{2,1,0:T(8,128)S(1)} custom-call(s32[64]{0:T(128)} %wave_scalar_ref.1, s32[1,64]{1,0:T(1,128)} %bitcast.3, bf16[2,320,5120]{2,1,0:T(8,128)(2,1)} %field_ref.1, bf16[8,2,160,1280]{3,2,1,0:T(8,128)(2,1)} %legendre_ref.1), custom_call_target="tpu_custom_call" | custom-call | tf_op jit(solution)/shard_map/pallas_call | solution.py:367
  21.1 0.7 %copy.5 = f32[8,160,32]{1,2,0:T(8,128)} copy(f32[8,160,32]{1,2,0:T(8,128)S(1)} %bitcast.2) | data formatting | bytes 327680
